TPU v7x, 32 devices: a whole 2x2x4 slice. The times are simulated.
32 devices in a mesh: pb: 8 (over y, x, core), row: 4 (over z).
Axes of the slice: x: 2, y: 2, z: 4, core: 2. Of those that a mesh axis runs over, the one named last changes fastest.
Arguments:
- valence_bands: bfloat16 [8, 20, 4096], P('pb', None, 'row'), may hold values from -0.75 to 0.75
- conduction_bands: bfloat16 [8, 20, 4096], P('pb', None, 'row'), may hold values from -6 to 6
- screened: bfloat16 [8, 4096, 4096], P('pb', 'row'), may hold values from -0.09375 to 0.09375
- pair_list: int32 [16, 2], replicated, may hold values from 0 to 7, as said below
- transfer_index: int32 [16, 1], replicated, may hold values from 0 to 7; in each aligned block of 16 rows (0 to 15, 16 to 31, ...) at most 6 rows name the same one
- owner_map: int32 [8], replicated, may hold values from 0 to 7, as said below
Outputs:
- direct: bfloat16 [16, 400, 400], P('pb', 'row')
- mirror: bfloat16 [16, 400, 400], P('pb', 'row')
Inputs may be any that keep to these rules, and one draw needn't show every extreme that they name: owner_map is a permutation of 0 to 7. `pair_list`: the two k-points of a pair differ. The first k-point of pairs e * 2 to e * 2 + 1 is the one that owner_map sends to e. Over all pairs, the second k-points are sent by owner_map to every value 0 to 7 exactly 2 times. `transfer_index`: at most 6 pairs share one momentum transfer, and some transfer has exactly 6; every transfer has at least one pair.
All inputs are finite; a program needn't handle non-finite values.
Results may differ from a plain program's by a relative error of at most 0.0065.
Values may be sent and summed in bfloat16 or wider, within the bound.
No kernel may reach another device: no remote copies, remote signals or barrier semaphores. Data moves between devices by JAX's collectives and lax.ppermute only.
A program may use at most 64 MiB of HBM per device.

v0:
```python
import jax
import jax.numpy as jnp
from jax import lax
from jax.sharding import PartitionSpec as P

PAIR_DEV = 2
MOST = 6


def rank_table(labels, groups, slots_per):
    total_rows = labels.shape[0]
    member = (labels[None, :] == jnp.arange(groups, dtype=jnp.int32)[:, None]).astype(jnp.int32)
    before = jnp.cumsum(member, axis=1) - 1
    placed = member[:, None, :] * (
        before[:, None, :] == jnp.arange(slots_per, dtype=jnp.int32)[None, :, None]
    ).astype(jnp.int32)
    numbers = jnp.arange(total_rows, dtype=jnp.int32) + 1
    return jnp.sum(placed * numbers[None, None, :], axis=2) - 1


def pair_kernel(val_first, val_second, con_first, con_second, screen_rows):
    val_count = val_first.shape[0]
    con_count = con_first.shape[0]
    val_pairs = val_first[:, None, :].astype(jnp.float32) * val_second[None, :, :].astype(
        jnp.float32
    )
    val_pairs = val_pairs.reshape(val_count * val_count, val_first.shape[1]).astype(jnp.bfloat16)
    con_pairs = con_first[:, None, :].astype(jnp.float32) * con_second[None, :, :].astype(
        jnp.float32
    )
    con_pairs = con_pairs.reshape(con_count * con_count, con_first.shape[1]).astype(jnp.bfloat16)
    interim = lax.dot_general(
        screen_rows, con_pairs, (((1,), (1,)), ((), ())), preferred_element_type=jnp.float32
    ).astype(jnp.bfloat16)
    partial_sum = jnp.dot(val_pairs, interim, preferred_element_type=jnp.float32)
    partial_sum = partial_sum.reshape(val_count, val_count, con_count, con_count).transpose(
        0, 2, 1, 3
    )
    return partial_sum.reshape(val_count * con_count, val_count * con_count)


def shards(valence_bands, conduction_bands, screened, pair_list, transfer_index, owner_map):
    groups = lax.axis_size("pb")
    rows_split = lax.axis_size("row")
    device = lax.axis_index("pb")
    val_all, con_local = (
        lax.all_gather(valence_bands, "pb", axis=0, tiled=True),
        lax.all_gather(conduction_bands, "pb", axis=0, tiled=True),
    )
    slot_table = rank_table(transfer_index[:, 0], groups, MOST)
    own_slots = lax.dynamic_index_in_dim(slot_table, device, 0, keepdims=False)
    live_pair = jnp.maximum(own_slots, 0)
    slot_first = jnp.take(owner_map, jnp.take(pair_list[:, 0], live_pair))
    slot_second = jnp.take(owner_map, jnp.take(pair_list[:, 1], live_pair))
    val_first = jnp.take(val_all, slot_first, axis=0)
    val_second = jnp.take(val_all, slot_second, axis=0)
    con_full = lax.all_gather(con_local, "row", axis=2, tiled=True)
    con_first = jnp.take(con_full, slot_first, axis=0)
    con_second = jnp.take(con_full, slot_second, axis=0)
    screen_rows = screened[0]

    def one_slot(operands):
        return pair_kernel(operands[0], operands[1], operands[2], operands[3], screen_rows)

    partials = lax.map(one_slot, (val_first, val_second, con_first, con_second))
    shares = lax.psum_scatter(partials, "row", scatter_dimension=1, tiled=True).astype(jnp.bfloat16)
    band_rows = shares.shape[1]
    mirror_table = rank_table(jnp.take(owner_map, pair_list[:, 1]), groups, PAIR_DEV)
    flat_slots = slot_table.reshape(-1)
    own_direct = device * PAIR_DEV + jnp.arange(PAIR_DEV, dtype=jnp.int32)
    own_mirror = lax.dynamic_index_in_dim(mirror_table, device, 0, keepdims=False)
    wanted = jnp.concatenate([own_direct, own_mirror])
    select = (wanted[:, None] == flat_slots[None, :]).astype(jnp.bfloat16)
    arrived = jnp.einsum(
        "ji,ixy->jxy",
        select,
        lax.all_gather(shares, "pb", axis=0, tiled=True),
        preferred_element_type=jnp.float32,
    )
    direct = arrived[:PAIR_DEV].astype(jnp.bfloat16)
    mirror_rows = arrived[PAIR_DEV:].astype(jnp.bfloat16)
    turned = jnp.transpose(mirror_rows, (0, 2, 1)).reshape(
        PAIR_DEV, rows_split, band_rows, band_rows
    )
    swapped = lax.all_to_all(turned, "row", split_axis=1, concat_axis=3, tiled=True)
    mirror = swapped.reshape(PAIR_DEV, band_rows, band_rows * rows_split)
    return (direct, mirror)


def solution(mesh):
    in_specs = (P("pb", None, "row"), P("pb", None, "row"), P("pb", "row", None), P(), P(), P())
    out_specs = (P("pb", "row", None), P("pb", "row", None))
    return jax.shard_map(shards, mesh=mesh, in_specs=in_specs, out_specs=out_specs, check_vma=False)
```

profile of v0, /device:TPU:0, one launch (start us, length us, event | category | flops | bytes accessed | tf_op | source)
XLA Modules:
  0.0 460.9 jit_solution(9152695233821279163)
XLA Ops:
  7.2 12.9 %all_gather.13 = bf16[8,20,1024]{2,1,0:T(8,128)(2,1)} all-gather(bf16[1,20,1024]{2,1,0:T(8,128)(2,1)} %param.17), channel_id=1, replica_groups=mesh['pb'=8,'row'=4] {'pb'}, dimensions={0}, use_global_device_ids=true | all-gather | bytes 368640 | tf_op jit(solution)/shard_map/all_gather | solution.py:48
  24.9 8.8 %all_gather.12 = bf16[8,20,1024]{2,1,0:T(8,128)(2,1)S(1)} all-gather(bf16[1,20,1024]{2,1,0:T(8,128)(2,1)} %param.16), channel_id=1, replica_groups=mesh['pb'=8,'row'=4] {'pb'}, dimensions={0}, use_global_device_ids=true | all-gather | bytes 368640 | tf_op jit(solution)/shard_map/all_gather | solution.py:47
  37.8 19.8 %all-gather.3.cloned.1.call-done = bf16[8,20,4096]{2,1,0:T(8,128)(2,1)} async-done(((bf16[8,20,1024]{2,1,0:T(8,128)(2,1)}), bf16[8,20,4096]{2,1,0:T(8,128)(2,1)}) %all-gather.3.cloned.1.call-update) | async-done | bytes 1310736 | tf_op jit(solution)/shard_map/all_gather | solution.py:57
  57.6 2.1 gather_fusion.8
  59.8 1.2 broadcast_select_fusion
  61.6 1.2 broadcast_select_fusion.1
  62.8 156.2 %while.10 = (s32[]{:T(128)}, f32[6,400,400]{1,2,0:T(8,128)}, bf16[6,20,1024]{2,1,0:T(8,128)(2,1)}, bf16[6,20,1024]{2,1,0:T(8,128)(2,1)}, bf16[6,20,4096]{2,1,0:T...) while((s32[]{:T(128)}, f32[6,400,400]{1,2,0:T(8,128)}, ...), condition=%wide.region_5.10_spmd, body=%wide.region_4.9_spmd.sunk | while | flops 3687833600 | bytes 31480412 | solution.py:65
  62.8 1.1 bitcast_convert_fusion.6
  63.9 2.6 multiply_convert_fusion.3
  66.5 3.9 convert_element_type.89
  70.4 7.0 %convolution_convert_fusion.3 = bf16[400,1024]{1,0:T(8,128)(2,1)} fusion(bf16[400,4096]{1,0:T(8,128)(2,1)S(1)} %convert_element_type.89, bf16[1024,4096]{1,0:T(8,128)(2,1)} %get-tuple-element.156), kind=kOutput, calls=%fused_computation.12.clone.1 | convolution fusion | flops 3355852800 | bytes 12484608 | tf_op jit(solution)/shard_map/while/body/eval_jaxpr/dot_general | solution.py:32
  77.4 1.2 reshape.284
  78.7 0.8 bitcast_convert_fusion.7
  79.5 4.5 convolution_bitcast_fusion.2
  84.0 3.6 broadcast_in_dim.75
  87.9 1.0 constant_dynamic-update-slice_fusion.2
  88.9 1.1 bitcast_convert_fusion.6
  89.9 2.6 multiply_convert_fusion.3
  92.6 3.9 convert_element_type.89
  96.4 7.0 %convolution_convert_fusion.3 = bf16[400,1024]{1,0:T(8,128)(2,1)} fusion(bf16[400,4096]{1,0:T(8,128)(2,1)S(1)} %convert_element_type.89, bf16[1024,4096]{1,0:T(8,128)(2,1)} %get-tuple-element.156), kind=kOutput, calls=%fused_computation.12.clone.1 | convolution fusion | flops 3355852800 | bytes 12484608 | tf_op jit(solution)/shard_map/while/body/eval_jaxpr/dot_general | solution.py:32
  103.5 1.2 reshape.284
  105.6 4.5 convolution_bitcast_fusion.2
  110.0 3.6 broadcast_in_dim.75
  113.9 1.0 constant_dynamic-update-slice_fusion.2
  114.9 1.1 bitcast_convert_fusion.6
  116.0 2.6 multiply_convert_fusion.3
  118.6 3.9 convert_element_type.89
  122.5 7.0 %convolution_convert_fusion.3 = bf16[400,1024]{1,0:T(8,128)(2,1)} fusion(bf16[400,4096]{1,0:T(8,128)(2,1)S(1)} %convert_element_type.89, bf16[1024,4096]{1,0:T(8,128)(2,1)} %get-tuple-element.156), kind=kOutput, calls=%fused_computation.12.clone.1 | convolution fusion | flops 3355852800 | bytes 12484608 | tf_op jit(solution)/shard_map/while/body/eval_jaxpr/dot_general | solution.py:32
  129.5 1.2 reshape.284
  131.6 4.5 convolution_bitcast_fusion.2
  136.0 3.6 broadcast_in_dim.75
  139.9 1.0 constant_dynamic-update-slice_fusion.2
  140.9 1.1 bitcast_convert_fusion.6
  142.0 2.6 multiply_convert_fusion.3
  144.6 3.9 convert_element_type.89
  148.5 7.0 %convolution_convert_fusion.3 = bf16[400,1024]{1,0:T(8,128)(2,1)} fusion(bf16[400,4096]{1,0:T(8,128)(2,1)S(1)} %convert_element_type.89, bf16[1024,4096]{1,0:T(8,128)(2,1)} %get-tuple-element.156), kind=kOutput, calls=%fused_computation.12.clone.1 | convolution fusion | flops 3355852800 | bytes 12484608 | tf_op jit(solution)/shard_map/while/body/eval_jaxpr/dot_general | solution.py:32
  155.5 1.2 reshape.284
  157.6 4.5 convolution_bitcast_fusion.2
  162.1 3.6 broadcast_in_dim.75
  166.0 1.0 constant_dynamic-update-slice_fusion.2
  167.0 1.1 bitcast_convert_fusion.6
  168.0 2.6 multiply_convert_fusion.3
  170.6 3.9 convert_element_type.89
  174.5 7.0 %convolution_convert_fusion.3 = bf16[400,1024]{1,0:T(8,128)(2,1)} fusion(bf16[400,4096]{1,0:T(8,128)(2,1)S(1)} %convert_element_type.89, bf16[1024,4096]{1,0:T(8,128)(2,1)} %get-tuple-element.156), kind=kOutput, calls=%fused_computation.12.clone.1 | convolution fusion | flops 3355852800 | bytes 12484608 | tf_op jit(solution)/shard_map/while/body/eval_jaxpr/dot_general | solution.py:32
  181.6 1.2 reshape.284
  183.7 4.5 convolution_bitcast_fusion.2
  188.1 3.6 broadcast_in_dim.75
  192.0 1.0 constant_dynamic-update-slice_fusion.2
  193.0 1.1 bitcast_convert_fusion.6
  194.0 2.6 multiply_convert_fusion.3
  196.7 3.9 convert_element_type.89
  200.5 7.0 %convolution_convert_fusion.3 = bf16[400,1024]{1,0:T(8,128)(2,1)} fusion(bf16[400,4096]{1,0:T(8,128)(2,1)S(1)} %convert_element_type.89, bf16[1024,4096]{1,0:T(8,128)(2,1)} %get-tuple-element.156), kind=kOutput, calls=%fused_computation.12.clone.1 | convolution fusion | flops 3355852800 | bytes 12484608 | tf_op jit(solution)/shard_map/while/body/eval_jaxpr/dot_general | solution.py:32
  207.6 1.2 reshape.284
  209.7 4.5 convolution_bitcast_fusion.2
  214.1 3.6 broadcast_in_dim.75
  218.0 1.0 constant_dynamic-update-slice_fusion.2
  219.0 169.8 %all-reduce.2 = bf16[6,400,400]{1,2,0:T(8,128)(2,1)S(1)} all-reduce(f32[6,400,400]{1,2,0:T(8,128)} %get-tuple-element.43), channel_id=2, replica_groups=mesh['pb'=8,'row'=4] {'row'}, use_global_device_ids=true, to_apply=%region_6.11.clone | all-reduce | flops 960000 | bytes 5760000
  388.8 1.1 dynamic-slice_convert_fusion
  391.4 36.1 %all-gather.5.cloned.1.call-done = bf16[48,100,400]{1,2,0:T(8,128)(2,1)} async-done(((bf16[6,100,400]{1,2,0:T(8,128)(2,1)}), bf16[48,100,400]{1,2,0:T(8,128)(2,1)}) %all-gather.5.cloned.1.call-update) | async-done | bytes 3840016 | tf_op jit(solution)/shard_map/all_gather | solution.py:77
  427.5 8.4 %copy.27 = bf16[48,100,400]{2,0,1:T(8,128)(2,1)} copy(bf16[48,100,400]{1,2,0:T(8,128)(2,1)} %all-gather.5.cloned.1.call-done) | data formatting | bytes 7680000 | tf_op jit(solution)/shard_map/all_gather | solution.py:77
  435.9 3.2 convolution_convert_fusion.1
  439.1 1.0 slice_bitcast_fusion
  440.4 12.5 %all_to_all.15 = bf16[2,4,100,100]{2,0,3,1:T(2,128)(2,1)S(1)} all-to-all(bf16[2,4,100,100]{2,0,3,1:T(2,128)(2,1)S(1)} %copy.28), channel_id=1, replica_groups=mesh['pb'=8,'row'=4] {'row'}, dimensions={1} | all-to-all | bytes 320000 | tf_op jit(solution)/shard_map/all_to_all | solution.py:85
  452.9 1.2 copy.29
  (65 shorter events, 16.5 us)
Async XLA Ops:
  7.2 16.4 %copy-start = (s32[8]{0:T(128)S(1)}, s32[8]{0:T(128)}, u32[]{:S(2)}) copy-start(s32[8]{0:T(128)} %param.21) | copy-start | bytes 100
  7.2 27.8 %copy-start.3 = (u32[32]{0:T(128)S(1)}, u32[32]{0:T(128)}, u32[]{:S(2)}) copy-start(u32[32]{0:T(128)} %constant.110) | copy-start | bytes 388
  7.2 50.4 %all-gather.3.cloned.1.call-start = ((), (), s32[]{:S(2)}) async-start(), calls=%async_computation.1 | async-start | bytes 1966080 | tf_op jit(solution)/shard_map/all_gather | solution.py:57
  20.2 407.3 %all-gather.5.cloned.1.call-start = ((), (), s32[]{:S(2)}) async-start(), calls=%async_computation.2 | async-start | bytes 5529600 | tf_op jit(solution)/shard_map/all_gather | solution.py:77
  57.6 3.4 copy-start.1
  219.0 171.7 %copy-start.2 = (s32[16,2]{0,1:T(2,128)S(1)}, s32[16,2]{0,1:T(2,128)}, u32[]{:S(2)}) copy-start(s32[16,2]{0,1:T(2,128)} %param.19) | copy-start | bytes 388
Sparse Core Ops, SparseCore 0:
  20.3 37.2 all-gather.2
  390.1 37.3 all-gather.4
where the time goes:
time: 463 us; the launch traced here: 461 us
  blocking collectives  204 us (44%)
  local copies, waits for them, and re-layouts  80 us (17%)
  matrix products  72.2 us (16%)
  waiting for transfers between devices  55.9 us (12%)
  other arithmetic  33.6 us (7%)
  between operations  14.9 us (3%)
    unnamed x1, blocking collectives  170 us
    dot_general x6, matrix products, pair_kernel(): lax.dot_general(screen_rows, con_pairs, (((1,), (1,)), ((), ())), preferr...  42.1 us
    all_gather x1, waiting for transfers between devices, shards(): lax.all_gather(shares, 'pb', axis=0, tiled=True)  36.1 us
    dot_general x6, matrix products, pair_kernel(): jnp.dot(val_pairs, interim, preferred_element_type=jnp.float32)  26.8 us
    convert_element_type x6, local copies, waits for them, and re-layouts, pair_kernel(): con_pairs.reshape(con_count * con_count, con_first.shape[1])  23.3 us
    broadcast_in_dim x6, local copies, waits for them, and re-layouts, shards(): partials = lax.map(one_slot, (val_first, val_second, con_first, con_second))  21.6 us
    all_gather x1, waiting for transfers between devices, shards(): con_full = lax.all_gather(con_local, 'row', axis=2, tiled=True)  19.8 us
    convert_element_type x6, other arithmetic, pair_kernel(): con_pairs.reshape(con_count * con_count, con_first.shape[1])  15.6 us
  transfers between devices with their start and end apart: 2, of which 2 were waited for; matrix products, arithmetic and copies ran while one was open for 2% of the time, Pallas kernels for 0%

commit v1 on v0

--- a/solution.py
+++ b/solution.py
@@ -71,12 +71,38 @@
     own_mirror = lax.dynamic_index_in_dim(mirror_table, device, 0, keepdims=False)
     wanted = jnp.concatenate([own_direct, own_mirror])
     select = (wanted[:, None] == flat_slots[None, :]).astype(jnp.bfloat16)
-    arrived = jnp.einsum(
+    count, mine, extent = (lax.axis_size("pb"), lax.axis_index("pb"), shares.shape[0])
+    right = [(i, (i + 1) % count) for i in range(count)]
+    backward = [(i, (i - 1) % count) for i in range(count)]
+    half = count // 2
+    from_left = from_right = shares
+    total = jnp.einsum(
         "ji,ixy->jxy",
-        select,
-        lax.all_gather(shares, "pb", axis=0, tiled=True),
+        lax.dynamic_slice_in_dim(select, mine * extent, shares.shape[0], axis=1),
+        shares,
         preferred_element_type=jnp.float32,
     )
+    for lap in range(1, half + 1):
+        from_left = lax.ppermute(from_left, "pb", right)
+        if lap < count - half:
+            from_right = lax.ppermute(from_right, "pb", backward)
+            total = total + jnp.einsum(
+                "ji,ixy->jxy",
+                lax.dynamic_slice_in_dim(
+                    select, (mine + lap) % count * extent, from_right.shape[0], axis=1
+                ),
+                from_right,
+                preferred_element_type=jnp.float32,
+            )
+        total = total + jnp.einsum(
+            "ji,ixy->jxy",
+            lax.dynamic_slice_in_dim(
+                select, (mine - lap) % count * extent, from_left.shape[0], axis=1
+            ),
+            from_left,
+            preferred_element_type=jnp.float32,
+        )
+    arrived = total
     direct = arrived[:PAIR_DEV].astype(jnp.bfloat16)
     mirror_rows = arrived[PAIR_DEV:].astype(jnp.bfloat16)
     turned = jnp.transpose(mirror_rows, (0, 2, 1)).reshape(

time: 463 us -> 478 us (1.032)
  starting transfers between devices: 0.08 us -> 6.3 us
  waiting for transfers between devices: 55.9 us -> 62.1 us
  local copies, waits for them, and re-layouts: 80 us -> 86.1 us
    ppermute x0 -> x7, waiting for transfers between devices: none -> 43.5 us  [the longest x4 43.5 us: shards(): from_left = lax.ppermute(from_left, 'pb', right)]
    all_gather x1 -> x0, waiting for transfers between devices: 36.1 us -> none  [shards(): lax.all_gather(shares, 'pb', axis=0, tiled=True)]
    ppermute x0 -> x7, local copies, waits for them, and re-layouts: none -> 14.1 us  [the longest x4 8.58 us: shards(): from_left = lax.ppermute(from_left, 'pb', right)]
    all_gather x1 -> x0, local copies, waits for them, and re-layouts: 8.41 us -> none  [shards(): lax.all_gather(shares, 'pb', axis=0, tiled=True)]
    ppermute x0 -> x7, starting transfers between devices: none -> 6.26 us  [the longest x3 5.41 us: shards(): from_right = lax.ppermute(from_right, 'pb', backward)]
  transfers between devices with their start and end apart: 2 -> 8, of which waited for: 2 -> 5; matrix products, arithmetic and copies ran while one was open for 2% -> 5% of each run, Pallas kernels for 0% -> 0%
where the time goes in v1:
time: 478 us; the launch traced here: 476 us
  blocking collectives  201 us (42%)
  local copies, waits for them, and re-layouts  86.1 us (18%)
  matrix products  72.4 us (15%)
  waiting for transfers between devices  62.1 us (13%)
  other arithmetic  33.8 us (7%)
  between operations  15.1 us (3%)
  starting transfers between devices  6.3 us (1%)
    unnamed x1, blocking collectives  170 us
    ppermute x4, waiting for transfers between devices, shards(): from_left = lax.ppermute(from_left, 'pb', right)  43.5 us
    dot_general x6, matrix products, pair_kernel(): lax.dot_general(screen_rows, con_pairs, (((1,), (1,)), ((), ())), preferr...  42.1 us
    dot_general x6, matrix products, pair_kernel(): jnp.dot(val_pairs, interim, preferred_element_type=jnp.float32)  26.7 us
    convert_element_type x6, local copies, waits for them, and re-layouts, pair_kernel(): con_pairs.reshape(con_count * con_count, con_first.shape[1])  23.3 us
    broadcast_in_dim x6, local copies, waits for them, and re-layouts, shards(): partials = lax.map(one_slot, (val_first, val_second, con_first, con_second))  21.6 us
    all_gather x1, waiting for transfers between devices, shards(): con_full = lax.all_gather(con_local, 'row', axis=2, tiled=True)  18.5 us
    convert_element_type x6, other arithmetic, pair_kernel(): con_pairs.reshape(con_count * con_count, con_first.shape[1])  15.7 us
  transfers between devices with their start and end apart: 8, of which 5 were waited for; matrix products, arithmetic and copies ran while one was open for 5% of the time, Pallas kernels for 0%

profile of v1, /device:TPU:0, one launch (start us, length us, event | category | flops | bytes accessed | tf_op | source)
XLA Modules:
  0.0 476.5 jit_solution(12604587060664882049)
XLA Ops:
  7.2 12.9 %all_gather.10 = bf16[8,20,1024]{2,1,0:T(8,128)(2,1)} all-gather(bf16[1,20,1024]{2,1,0:T(8,128)(2,1)} %param.17), channel_id=1, replica_groups=mesh['pb'=8,'row'=4] {'pb'}, dimensions={0}, use_global_device_ids=true | all-gather | bytes 368640 | tf_op jit(solution)/shard_map/all_gather | solution.py:48
  24.9 8.7 %all_gather.9 = bf16[8,20,1024]{2,1,0:T(8,128)(2,1)S(1)} all-gather(bf16[1,20,1024]{2,1,0:T(8,128)(2,1)S(1)} %copy-done.2), channel_id=1, replica_groups=mesh['pb'=8,'row'=4] {'pb'}, dimensions={0}, use_global_device_ids=true | all-gather | bytes 368640 | tf_op jit(solution)/shard_map/all_gather | solution.py:47
  39.1 18.5 %all-gather.2.cloned.1.call-done = bf16[8,20,4096]{2,1,0:T(8,128)(2,1)} async-done(((bf16[8,20,1024]{2,1,0:T(8,128)(2,1)}), bf16[8,20,4096]{2,1,0:T(8,128)(2,1)}) %all-gather.2.cloned.1.call-update) | async-done | bytes 1310736 | tf_op jit(solution)/shard_map/all_gather | solution.py:57
  57.6 2.1 gather_fusion.8
  59.8 1.2 broadcast_select_fusion
  61.6 1.2 broadcast_select_fusion.1
  62.8 156.1 %while.10 = (s32[]{:T(128)}, f32[6,400,400]{1,2,0:T(8,128)}, bf16[6,20,1024]{2,1,0:T(8,128)(2,1)}, bf16[6,20,1024]{2,1,0:T(8,128)(2,1)}, bf16[6,20,4096]{2,1,0:T...) while((s32[]{:T(128)}, f32[6,400,400]{1,2,0:T(8,128)}, ...), condition=%wide.region_5.10_spmd, body=%wide.region_4.9_spmd.sunk | while | flops 3687833600 | bytes 31480412 | solution.py:65
  62.8 1.1 bitcast_convert_fusion.6
  63.9 2.6 multiply_convert_fusion.3
  66.5 3.9 convert_element_type.89
  70.4 7.0 %convolution_convert_fusion.2 = bf16[400,1024]{1,0:T(8,128)(2,1)} fusion(bf16[400,4096]{1,0:T(8,128)(2,1)S(1)} %convert_element_type.89, bf16[1024,4096]{1,0:T(8,128)(2,1)} %get-tuple-element.156), kind=kOutput, calls=%fused_computation.12.clone.1 | convolution fusion | flops 3355852800 | bytes 12484608 | tf_op jit(solution)/shard_map/while/body/eval_jaxpr/dot_general | solution.py:32
  77.4 1.2 reshape.291
  79.5 4.4 convolution_bitcast_fusion.2
  84.0 3.6 broadcast_in_dim.75
  88.8 1.1 bitcast_convert_fusion.6
  89.9 2.6 multiply_convert_fusion.3
  92.5 3.9 convert_element_type.89
  96.4 7.0 %convolution_convert_fusion.2 = bf16[400,1024]{1,0:T(8,128)(2,1)} fusion(bf16[400,4096]{1,0:T(8,128)(2,1)S(1)} %convert_element_type.89, bf16[1024,4096]{1,0:T(8,128)(2,1)} %get-tuple-element.156), kind=kOutput, calls=%fused_computation.12.clone.1 | convolution fusion | flops 3355852800 | bytes 12484608 | tf_op jit(solution)/shard_map/while/body/eval_jaxpr/dot_general | solution.py:32
  103.4 1.2 reshape.291
  105.5 4.5 convolution_bitcast_fusion.2
  110.0 3.6 broadcast_in_dim.75
  114.9 1.1 bitcast_convert_fusion.6
  115.9 2.6 multiply_convert_fusion.3
  118.5 3.9 convert_element_type.89
  122.4 7.0 %convolution_convert_fusion.2 = bf16[400,1024]{1,0:T(8,128)(2,1)} fusion(bf16[400,4096]{1,0:T(8,128)(2,1)S(1)} %convert_element_type.89, bf16[1024,4096]{1,0:T(8,128)(2,1)} %get-tuple-element.156), kind=kOutput, calls=%fused_computation.12.clone.1 | convolution fusion | flops 3355852800 | bytes 12484608 | tf_op jit(solution)/shard_map/while/body/eval_jaxpr/dot_general | solution.py:32
  129.5 1.2 reshape.291
  131.6 4.4 convolution_bitcast_fusion.2
  136.0 3.6 broadcast_in_dim.75
  141.9 2.6 multiply_convert_fusion.3
  144.5 3.9 convert_element_type.89
  148.4 7.0 %convolution_convert_fusion.2 = bf16[400,1024]{1,0:T(8,128)(2,1)} fusion(bf16[400,4096]{1,0:T(8,128)(2,1)S(1)} %convert_element_type.89, bf16[1024,4096]{1,0:T(8,128)(2,1)} %get-tuple-element.156), kind=kOutput, calls=%fused_computation.12.clone.1 | convolution fusion | flops 3355852800 | bytes 12484608 | tf_op jit(solution)/shard_map/while/body/eval_jaxpr/dot_general | solution.py:32
  155.5 1.2 reshape.291
  157.6 4.4 convolution_bitcast_fusion.2
  162.0 3.6 broadcast_in_dim.75
  167.9 2.6 multiply_convert_fusion.3
  170.6 3.9 convert_element_type.89
  174.4 7.0 %convolution_convert_fusion.2 = bf16[400,1024]{1,0:T(8,128)(2,1)} fusion(bf16[400,4096]{1,0:T(8,128)(2,1)S(1)} %convert_element_type.89, bf16[1024,4096]{1,0:T(8,128)(2,1)} %get-tuple-element.156), kind=kOutput, calls=%fused_computation.12.clone.1 | convolution fusion | flops 3355852800 | bytes 12484608 | tf_op jit(solution)/shard_map/while/body/eval_jaxpr/dot_general | solution.py:32
  181.5 1.2 reshape.291
  183.6 4.5 convolution_bitcast_fusion.2
  188.0 3.6 broadcast_in_dim.75
  192.9 1.1 bitcast_convert_fusion.6
  194.0 2.6 multiply_convert_fusion.3
  196.6 3.9 convert_element_type.89
  200.5 7.0 %convolution_convert_fusion.2 = bf16[400,1024]{1,0:T(8,128)(2,1)} fusion(bf16[400,4096]{1,0:T(8,128)(2,1)S(1)} %convert_element_type.89, bf16[1024,4096]{1,0:T(8,128)(2,1)} %get-tuple-element.156), kind=kOutput, calls=%fused_computation.12.clone.1 | convolution fusion | flops 3355852800 | bytes 12484608 | tf_op jit(solution)/shard_map/while/body/eval_jaxpr/dot_general | solution.py:32
  207.5 1.2 reshape.291
  209.6 4.5 convolution_bitcast_fusion.2
  214.1 3.6 broadcast_in_dim.75
  218.9 169.8 %all-reduce.2 = bf16[6,400,400]{1,2,0:T(8,128)(2,1)S(1)} all-reduce(f32[6,400,400]{1,2,0:T(8,128)} %get-tuple-element.43), channel_id=2, replica_groups=mesh['pb'=8,'row'=4] {'row'}, use_global_device_ids=true, to_apply=%region_6.11.clone | all-reduce | flops 960000 | bytes 5760000
  389.6 1.2 copy.48
  391.2 13.9 %collective-permute-done.1 = bf16[6,100,400]{1,2,0:T(8,128)(2,1)} collective-permute-done((bf16[6,100,400]{1,2,0:T(8,128)(2,1)S(1)}, bf16[6,100,400]{1,2,0:T(8,128)(2,1)}, u32[]{:S(2)}, u32[]{:S(2)}) %collective-permute-start.1) | collective-permute-done | bytes 480032 | tf_op jit(solution)/shard_map/ppermute | solution.py:86
  405.1 2.1 copy.50
  407.5 2.1 copy.49
  409.7 2.7 collective-permute-start.2
  413.3 9.4 %collective-permute-done.3 = bf16[6,100,400]{1,2,0:T(8,128)(2,1)} collective-permute-done((bf16[6,100,400]{1,2,0:T(8,128)(2,1)}, bf16[6,100,400]{1,2,0:T(8,128)(2,1)}, u32[]{:S(2)}, u32[]{:S(2)}) %collective-permute-start.3) | collective-permute-done | bytes 480032 | tf_op jit(solution)/shard_map/ppermute | solution.py:86
  422.7 2.1 copy.52
  424.9 1.2 copy.51
  426.2 2.7 collective-permute-start.4
  429.8 12.5 %collective-permute-done.5 = bf16[6,100,400]{1,2,0:T(8,128)(2,1)} collective-permute-done((bf16[6,100,400]{1,2,0:T(8,128)(2,1)}, bf16[6,100,400]{1,2,0:T(8,128)(2,1)}, u32[]{:S(2)}, u32[]{:S(2)}) %collective-permute-start.5) | collective-permute-done | bytes 480032 | tf_op jit(solution)/shard_map/ppermute | solution.py:86
  442.3 2.1 copy.54
  444.5 2.1 copy.53
  447.6 7.7 %collective-permute-done.6 = bf16[6,100,400]{1,2,0:T(8,128)(2,1)} collective-permute-done((bf16[6,100,400]{1,2,0:T(8,128)(2,1)}, bf16[6,100,400]{1,2,0:T(8,128)(2,1)}, u32[]{:S(2)}, u32[]{:S(2)}) %collective-permute-start.6) | collective-permute-done | bytes 480032 | tf_op jit(solution)/shard_map/ppermute | solution.py:86
  455.2 2.1 copy.55
  459.2 9.2 %all_to_all.15 = bf16[2,4,100,100]{2,0,3,1:T(2,128)(2,1)S(1)} all-to-all(bf16[2,4,100,100]{2,0,3,1:T(2,128)(2,1)S(1)} %copy.56), channel_id=1, replica_groups=mesh['pb'=8,'row'=4] {'row'}, dimensions={1} | all-to-all | bytes 320000 | tf_op jit(solution)/shard_map/all_to_all | solution.py:111
  468.4 1.2 copy.57
  (93 shorter events, 31.0 us)
Async XLA Ops:
  7.2 16.4 %copy-start = (s32[8]{0:T(128)S(1)}, s32[8]{0:T(128)}, u32[]{:S(2)}) copy-start(s32[8]{0:T(128)} %param.21) | copy-start | bytes 100
  7.2 17.7 %copy-start.2 = (bf16[1,20,1024]{2,1,0:T(8,128)(2,1)S(1)}, bf16[1,20,1024]{2,1,0:T(8,128)(2,1)}, u32[]{:S(2)}) copy-start(bf16[1,20,1024]{2,1,0:T(8,128)(2,1)} %param.16) | copy-start | bytes 122884
  7.2 50.4 %all-gather.2.cloned.1.call-start = ((), (), s32[]{:S(2)}) async-start(), calls=%async_computation.1 | async-start | bytes 1966080 | tf_op jit(solution)/shard_map/all_gather | solution.py:57
  22.8 12.6 %copy-start.3 = (s32[16,2]{0,1:T(2,128)S(1)}, s32[16,2]{0,1:T(2,128)}, u32[]{:S(2)}) copy-start(s32[16,2]{0,1:T(2,128)} %param.19) | copy-start | bytes 388
  22.8 13.3 %copy-start.4 = (u32[32]{0:T(128)S(1)}, u32[32]{0:T(128)}, u32[]{:S(2)}) copy-start(u32[32]{0:T(128)} %constant.159) | copy-start | bytes 388
  57.6 3.4 copy-start.1
  388.9 18.6 %collective-permute-start = (bf16[6,100,400]{1,2,0:T(8,128)(2,1)S(1)}, bf16[6,100,400]{1,2,0:T(8,128)(2,1)}, u32[]{:S(2)}, u32[]{:S(2)}) collective-permute-start(bf16[6,100,400]{1,2,0:T(8,128)(2,1)S(1)} %dynamic-slice_convert_fusion), channel_id=1, source_target_pairs={{0,28},{4,0},{8,4},{12,8},{16,12},{20,16},{24,20},{28,24},{1,29},{... | collective-permute-start | bytes 1440008 | tf_op jit(solution)/shard_map/ppermute | solution.py:88
  389.0 16.1 %collective-permute-start.1 = (bf16[6,100,400]{1,2,0:T(8,128)(2,1)S(1)}, bf16[6,100,400]{1,2,0:T(8,128)(2,1)}, u32[]{:S(2)}, u32[]{:S(2)}) collective-permute-start(bf16[6,100,400]{1,2,0:T(8,128)(2,1)S(1)} %dynamic-slice_convert_fusion), channel_id=1, source_target_pairs={{0,4},{4,8},{8,12},{12,16},{16,20},{20,24},{24,28},{28,0},{1,5},{5... | collective-permute-start | bytes 1440008 | tf_op jit(solution)/shard_map/ppermute | solution.py:86
  407.3 15.4 %collective-permute-start.3 = (bf16[6,100,400]{1,2,0:T(8,128)(2,1)}, bf16[6,100,400]{1,2,0:T(8,128)(2,1)}, u32[]{:S(2)}, u32[]{:S(2)}) collective-permute-start(bf16[6,100,400]{1,2,0:T(8,128)(2,1)} %collective-permute-done.1), channel_id=1, source_target_pairs={{0,4},{4,8},{8,12},{12,16},{16,20},{20,24},{24,28},{28,0},{1,5},{5... | collective-permute-start | bytes 1440008 | tf_op jit(solution)/shard_map/ppermute | solution.py:86
  409.7 15.2 %collective-permute-start.2 = (bf16[6,100,400]{1,2,0:T(8,128)(2,1)}, bf16[6,100,400]{1,2,0:T(8,128)(2,1)S(1)}, u32[]{:S(2)}, u32[]{:S(2)}) collective-permute-start(bf16[6,100,400]{1,2,0:T(8,128)(2,1)} %collective-permute-done), channel_id=1, source_target_pairs={{0,28},{4,0},{8,4},{12,8},{16,12},{20,16},{24,20},{28,24},{1,29},{... | collective-permute-start | bytes 1440008 | tf_op jit(solution)/shard_map/ppermute | solution.py:88
  424.9 17.4 %collective-permute-start.5 = (bf16[6,100,400]{1,2,0:T(8,128)(2,1)}, bf16[6,100,400]{1,2,0:T(8,128)(2,1)}, u32[]{:S(2)}, u32[]{:S(2)}) collective-permute-start(bf16[6,100,400]{1,2,0:T(8,128)(2,1)} %collective-permute-done.3), channel_id=1, source_target_pairs={{0,4},{4,8},{8,12},{12,16},{16,20},{20,24},{24,28},{28,0},{1,5},{5... | collective-permute-start | bytes 1440008 | tf_op jit(solution)/shard_map/ppermute | solution.py:86
  426.2 18.3 %collective-permute-start.4 = (bf16[6,100,400]{1,2,0:T(8,128)(2,1)S(1)}, bf16[6,100,400]{1,2,0:T(8,128)(2,1)}, u32[]{:S(2)}, u32[]{:S(2)}) collective-permute-start(bf16[6,100,400]{1,2,0:T(8,128)(2,1)S(1)} %collective-permute-done.2), channel_id=1, source_target_pairs={{0,28},{4,0},{8,4},{12,8},{16,12},{20,16},{24,20},{28,24},{1,29},{... | collective-permute-start | bytes 1440008 | tf_op jit(solution)/shard_map/ppermute | solution.py:88
  444.4 10.8 %collective-permute-start.6 = (bf16[6,100,400]{1,2,0:T(8,128)(2,1)}, bf16[6,100,400]{1,2,0:T(8,128)(2,1)}, u32[]{:S(2)}, u32[]{:S(2)}) collective-permute-start(bf16[6,100,400]{1,2,0:T(8,128)(2,1)} %collective-permute-done.5), channel_id=1, source_target_pairs={{0,4},{4,8},{8,12},{12,16},{16,20},{20,24},{24,28},{28,0},{1,5},{5... | collective-permute-start | bytes 1440008 | tf_op jit(solution)/shard_map/ppermute | solution.py:86
Sparse Core Ops, SparseCore 0:
  20.3 37.2 all-gather.1
